TPU v7x, 32 devices: a whole 2x2x4 slice. The times are simulated.
32 devices in a mesh: groups: 2 (over x), width: 8 (over z, y), guide: 2 (over core).
Axes of the slice: x: 2, y: 2, z: 4, core: 2. Of those that a mesh axis runs over, the one named last changes fastest.
Arguments:
- latent: float32 [16, 8, 2048], P(None, None, ('groups', 'width')), parts along dimension 2, may hold values from -6 to 6
- starts: int32 [16], P(('groups', 'width')), parts along dimension 0, may hold values from 0 to 1023, as said below
- counts: int32 [2048], P(('groups', 'width')), parts along dimension 0, may hold values from 1 to 3, as said below
- step_index: int32 [2], P('groups'), parts along dimension 0, may hold values from 0 to 27
- cond_mod: float32 [2, 3, 2432], P('guide'), may hold values from -3 to 3
- w_patch: bfloat16 [64, 2432], replicated, may hold values from -0.75 to 0.75
- w_qkv: bfloat16 [2432, 3840], P('width'), may hold values from -0.125 to 0.125
- w_out: bfloat16 [1280, 2432], replicated, may hold values from -0.15625 to 0.15625
- w_final: bfloat16 [2432, 64], replicated, may hold values from -0.125 to 0.125
- w_dec: bfloat16 [144, 512], replicated, may hold values from -0.5 to 0.5
Outputs:
- denoised: float32 [16, 8, 2048], P(None, 'guide', ('groups', 'width')), parts along dimension 2
- features: bfloat16 [8, 2048, 512], P('guide', ('groups', 'width')), parts along dimension 1
There are 2 independent parts, one for each index of `groups`. A program takes and returns all parts, laid end to end along the dimension named above; an argument that names none is the same for every part. Nothing has to cross between parts.
Inputs may be any that keep to these rules, and one draw needn't show every extreme that they name: window k starts between column k * 128 and column (k + 1) * 128 - 1 and covers 2 * 128 columns, wrapping around the panorama. `counts`: the number of windows whose columns, as given by starts, include the column.
All inputs are finite; a program needn't handle non-finite values.
Results may differ from a plain program's by a relative error of at most 0.013.
Values may be sent and summed in bfloat16 or wider, within the bound.
A program may use at most 128 MiB of HBM per device.

v0:
```python
import jax
import jax.numpy as jnp
from jax import lax
from jax.sharding import PartitionSpec as P

HEAD = 64
STEPS = 28
guidance = 4.0
epsilon = 1e-06


def from_behind(x, axis, by):
    peers = lax.axis_size(axis)
    return lax.ppermute(x, axis, [(i, (i + by) % peers) for i in range(peers)])


def from_partner(block, axis, stride):
    count = lax.axis_size(axis)
    route = []
    for low in range(count):
        high = low | 1 << stride
        if high != low and high < count:
            route += [(low, high), (high, low)]
    return lax.ppermute(block, axis, route)


def extended(block, sides, width):
    for axis, dim in sides:
        count = lax.axis_size(axis)
        forward = [(i, i + 1) for i in range(count - 1)]
        backward = [(target, source) for source, target in forward]
        low = lax.ppermute(
            lax.slice_in_dim(block, block.shape[dim] - width, None, axis=dim), axis, forward
        )
        high = lax.ppermute(lax.slice_in_dim(block, 0, width, axis=dim), axis, backward)
        block = jnp.concatenate([low, block, high], axis=dim)
    return block


def layer_norm(values):
    centered = values - jnp.mean(values, axis=-1, keepdims=True)
    spread = jnp.mean(centered * centered, axis=-1, keepdims=True)
    return centered * lax.rsqrt(spread + epsilon)


def head_norm(values):
    return values * lax.rsqrt(jnp.mean(values * values, axis=-1, keepdims=True) + epsilon)


def patchify(window):
    channels, height, breadth = window.shape
    folded = window.reshape(channels, height // 2, 2, breadth // 2, 2).transpose(1, 3, 2, 4, 0)
    return folded.reshape(height // 2 * (breadth // 2), 4 * channels)


def unpatchify(tokens, channels, height, breadth):
    folded = tokens.reshape(height // 2, breadth // 2, 2, 2, channels).transpose(4, 0, 2, 1, 3)
    return folded.reshape(channels, height, breadth)


def attend(queries, key_rows, value_rows):
    scores = jnp.einsum("bqhe,bkhe->bhqk", queries, key_rows, preferred_element_type=jnp.float32)
    scores = scores / jnp.sqrt(jnp.float32(queries.shape[-1]))
    weights = jax.nn.softmax(scores, axis=-1).astype(jnp.bfloat16)
    mixed = jnp.einsum("bhqk,bkhe->bqhe", weights, value_rows, preferred_element_type=jnp.float32)
    return mixed.astype(jnp.bfloat16)


def convolve(padded, w_dec):
    channels = padded.shape[0]
    height = padded.shape[1] - 2
    breadth = padded.shape[2] - 2
    shifted = [
        padded[:, row_at : row_at + height, col_at : col_at + breadth]
        for row_at in range(3)
        for col_at in range(3)
    ]
    stacked = jnp.stack(shifted).reshape(9 * channels, height * breadth)
    summed = lax.dot_general(
        stacked, w_dec, (((0,), (0,)), ((), ())), preferred_element_type=jnp.float32
    )
    return jax.nn.silu(summed).astype(jnp.bfloat16).reshape(height, breadth, w_dec.shape[1])


def halves(values):
    high = lax.reduce_precision(values, 8, 7)
    return (high.astype(jnp.bfloat16), (values - high).astype(jnp.bfloat16))


def fold(modulation, w_patch, w_qkv, place):
    patch = w_patch.astype(jnp.float32)
    patch = patch - jnp.mean(patch, axis=1, keepdims=True)
    rows = jnp.concatenate([patch * (1.0 + modulation[1]), modulation[0:1]], axis=0)
    depth = w_qkv.shape[0]
    rows = lax.dynamic_slice_in_dim(rows, place * depth, depth, 1)
    high, low = halves(rows)
    both = jnp.dot(jnp.concatenate([high, low], axis=0), w_qkv, preferred_element_type=jnp.float32)
    return both[: rows.shape[0]] + both[rows.shape[0] :]


def fetch_next(block):
    return from_behind(block, "width", -1)


def pass_right(block):
    return from_behind(block.astype(jnp.bfloat16), "width", 1).astype(block.dtype)


def shards(latent, starts, counts, step_index, cond_mod, w_patch, w_qkv, w_out, w_final, w_dec):
    guide_at = lax.axis_index("guide")
    place = lax.axis_index("width")
    channels, height, columns = latent.shape
    half_rows = height // 2
    fraction = (step_index[0].astype(jnp.float32) + 1.0) / STEPS
    sigma = 3.0 * fraction / (1.0 + 2.0 * fraction)
    modulation = cond_mod[0]
    own_cols = latent.astype(jnp.bfloat16)
    ahead = fetch_next(own_cols)
    further = fetch_next(ahead)
    three_blocks = jnp.concatenate([own_cols, ahead, further], axis=2)
    offset = starts[0] - place * columns
    window = lax.dynamic_slice_in_dim(three_blocks, offset, 2 * columns, 2)
    patches = patchify(window)
    token_count = patches.shape[0]
    hidden = jnp.dot(patches, w_patch, preferred_element_type=jnp.float32)
    centered = hidden - jnp.mean(hidden, axis=-1, keepdims=True)
    rstd = lax.rsqrt(jnp.mean(centered * centered, axis=-1, keepdims=True) + epsilon)
    heads = w_qkv.shape[1] // (3 * HEAD)
    folded = lax.psum(fold(modulation, w_patch, w_qkv, place), "width")
    patch_rows = w_patch.shape[0]
    high, low = halves(folded[:patch_rows])
    projected = jnp.dot(
        jnp.concatenate([patches, patches], axis=1),
        jnp.concatenate([high, low], axis=0),
        preferred_element_type=jnp.float32,
    )
    projected = projected * rstd + folded[patch_rows : patch_rows + 1]
    projected = projected.reshape(token_count, 3, heads, HEAD)
    queries = head_norm(projected[:, 0]).astype(jnp.bfloat16)
    key_rows = head_norm(projected[:, 1]).astype(jnp.bfloat16)
    value_rows = projected[:, 2].astype(jnp.bfloat16)
    attended = attend(queries[None], key_rows[None], value_rows[None])[0]
    attended = attended.reshape(token_count, heads * HEAD)
    mixed_out = jnp.dot(attended, w_out, preferred_element_type=jnp.float32)
    residual = hidden + modulation[2] * mixed_out
    final_in = layer_norm(residual).astype(jnp.bfloat16)
    result = jnp.dot(final_in, w_final, preferred_element_type=jnp.float32)
    velocity_win = unpatchify(result, channels, height, 2 * columns)
    branch_pair = lax.all_to_all(
        velocity_win[None].astype(jnp.bfloat16), "guide", split_axis=2, concat_axis=0, tiled=True
    ).astype(jnp.float32)
    guided = branch_pair[1] + guidance * (branch_pair[0] - branch_pair[1])
    spread_out = jnp.zeros((channels, half_rows, 3 * columns), jnp.float32)
    spread_out = lax.dynamic_update_slice_in_dim(spread_out, guided, offset, 2)
    carried = pass_right(spread_out[:, :, 2 * columns :])
    arrived = pass_right(spread_out[:, :, columns : 2 * columns] + carried)
    summed = spread_out[:, :, :columns] + arrived
    velocity = summed / counts.astype(jnp.float32)[None, None, :]
    mine_rows = lax.dynamic_slice_in_dim(latent, guide_at * half_rows, half_rows, 1)
    denoised = mine_rows - sigma * velocity
    padded = extended(denoised.astype(jnp.bfloat16), (("guide", 1), ("width", 2)), 1)
    features = convolve(padded, w_dec)
    return (denoised, features)


def solution(mesh):
    return jax.shard_map(
        shards,
        mesh=mesh,
        in_specs=(
            P(None, None, ("groups", "width")),
            P(("groups", "width")),
            P(("groups", "width")),
            P("groups"),
            P("guide", None, None),
            P(),
            P("width", None),
            P(),
            P(),
            P(),
        ),
        out_specs=(P(None, "guide", ("groups", "width")), P("guide", ("groups", "width"), None)),
        check_vma=False,
    )
```

profile of v0, /device:TPU:0, one launch (start us, length us, event | category | flops | bytes accessed | tf_op | source)
XLA Modules:
  0.0 190.0 jit_solution(14800418378556094931)
XLA Ops:
  7.2 1.0 convert_element_type.102
  8.2 6.0 %collective-permute-start = (bf16[16,8,128]{2,1,0:T(8,128)(2,1)S(1)}, bf16[16,8,128]{2,1,0:T(8,128)(2,1)S(1)}, u32[]{:S(2)}, u32[]{:S(2)}) collective-permute-start(bf16[16,8,128]{2,1,0:T(8,128)(2,1)S(1)} %convert_element_type.102), channel_id=1, source_target_pairs={{0,14},{2,0},{4,2},{6,4},{8,6},{10,8},{12,10},{14,12},{1,15},{3,1}... | collective-permute-start | bytes 98312 | tf_op jit(solution)/shard_map/ppermute | solution.py:14
  14.3 0.8 slice_reduce_fusion.1
  15.0 1.1 convert_reduce_fusion
  16.2 1.1 fusion.20
  17.3 0.1 reduce-precision_convert_fusion.1
  17.4 0.7 fusion.29
  18.1 2.7 %collective-permute-start.1 = (bf16[16,8,128]{2,1,0:T(8,128)(2,1)S(1)}, bf16[16,8,128]{2,1,0:T(8,128)(2,1)S(1)}, u32[]{:S(2)}, u32[]{:S(2)}) collective-permute-start(bf16[16,8,128]{2,1,0:T(8,128)(2,1)S(1)} %collective-permute-done), channel_id=1, source_target_pairs={{0,14},{2,0},{4,2},{6,4},{8,6},{10,8},{12,10},{14,12},{1,15},{3,1}... | collective-permute-start | bytes 98312 | tf_op jit(solution)/shard_map/ppermute | solution.py:14
  20.9 1.2 slice_add_fusion
  22.7 0.1 fusion.34
  22.9 0.3 copy.24
  23.1 0.4 copy.25
  23.6 0.9 fusion.51
  24.5 2.2 %copy-done.1 = f32[512,2432]{1,0:T(8,128)} copy-done((f32[512,2432]{1,0:T(8,128)}, f32[512,2432]{1,0:T(8,128)S(1)}, u32[]{:S(2)}) %copy-start.1) | copy-done | bytes 4980760
  26.7 0.6 multiply_reduce_fusion.2
  27.3 71.3 %all-reduce.2.cloned.1.call-done = f32[65,3840]{1,0:T(8,128)} async-done(((f32[65,3840]{1,0:T(8,128)}), f32[65,3840]{1,0:T(8,128)}) %all-reduce.2.cloned.1.call-update) | async-done | bytes 998416 | tf_op jit(solution)/shard_map/psum | solution.py:129
  98.6 1.3 reduce-precision_convert_fusion
  99.9 0.9 slice_reduce_fusion
  100.9 4.3 %multiply_add_fusion = f32[512,3840]{1,0:T(8,128)} fusion(f32[3840]{0:T(1024)S(1)} %slice_reduce_fusion, f32[512]{0:T(512)S(1)} %add_rsqrt_fusion.3, bf16[64,3840]{1,0:T(8,128)(2,1)S(1)} %get-tuple-element.9, bf16[64,3840]{1,0:T(8,128)(2,1)S(1)} %get-tuple-element.8, bf16[512,64]{0,1:T(8,128)(2,1)S(1)} %bitcast.139), kind=kOutput, calls=%fused_computation.7 | convolution fusion | flops 509476864 | bytes 8930304 | tf_op jit(solution)/shard_map/dot_general | solution.py:132
  105.2 9.1 %copy.26 = f32[512,3840]{0,1:T(8,128)} copy(f32[512,3840]{1,0:T(8,128)} %multiply_add_fusion) | data formatting | bytes 15728640 | tf_op jit(solution)/shard_map/add | solution.py:137
  114.2 3.3 %multiply_reduce_fusion.3 = (f32[512,20]{0,1:T(8,128)S(1)}, f32[512,20]{0,1:T(8,128)S(1)}) fusion(f32[512,3,20,64]{0,3,2,1:T(8,128)} %bitcast.131), kind=kLoop, calls=%fused_computation.18 | loop fusion | flops 2600960 | bytes 5324800 | tf_op jit(solution)/shard_map/reduce_sum | solution.py:47
  117.6 12.8 %fusion.52 = (f32[20,512]{1,0:T(8,128)S(1)}, f32[20,512,512]{1,2,0:T(8,128)}) fusion(f32[512,3,20,64]{0,3,2,1:T(8,128)} %bitcast.132, f32[512,20]{0,1:T(8,128)S(1)} %get-tuple-element.26, f32[512,20]{0,1:T(8,128)S(1)} %get-tuple-element.25), kind=kOutput, calls=%fused_computation.118 | convolution fusion | flops 689439232 | bytes 26337280 | tf_op jit(solution)/shard_map/sub | solution.py:64
  130.4 9.9 %fusion.12 = bf16[20,64,512]{2,1,0:T(8,128)(2,1)S(1)} fusion(f32[20,512,512]{1,2,0:T(8,128)} %get-tuple-element.22, f32[20,512]{1,0:T(8,128)S(1)} %get-tuple-element.21, f32[512,3,20,64]{0,3,2,1:T(8,128)} %bitcast.133), kind=kOutput, calls=%fused_computation.24 | convolution fusion | flops 682229760 | bytes 23633920 | tf_op jit(solution)/shard_map/bhqk,bkhe->bqhe/dot_general | solution.py:65
  140.3 6.3 %fusion.53 = (f32[512]{0:T(512)S(1)}, f32[512,2432]{1,0:T(8,128)S(1)}) fusion(f32[512,2432]{1,0:T(8,128)S(1)} %bitcast.130, bf16[512,1280]{0,1:T(8,128)(2,1)S(1)} %bitcast.136, bf16[1280,2432]{1,0:T(8,128)(2,1)} %param.17, f32[2432]{0:T(1024)S(1)} %get-tuple-element.4), kind=kOutput, calls=%fused_computation.119 | convolution fusion | flops 3191406080 | bytes 17509888 | tf_op jit(solution)/shard_map/dot_general | solution.py:144
  146.6 0.6 multiply_reduce_fusion.1
  147.3 0.3 copy-done.3
  147.6 1.1 fusion.15
  148.7 0.4 copy.28
  149.2 0.2 copy.29
  149.3 3.8 %all_to_all.4 = bf16[1,16,8,256]{3,1,0,2:T(8,128)(2,1)S(1)} all-to-all(bf16[1,16,8,256]{3,1,0,2:T(8,128)(2,1)S(1)} %copy.29), channel_id=1, replica_groups=mesh['groups'=2,'width'=8,'guide'=2] {'guide'}, dimensions={2} | all-to-all | bytes 131072 | tf_op jit(solution)/shard_map/all_to_all | solution.py:149
  153.3 2.6 %dynamic_update_slice.3 = f32[16,4,384]{2,1,0:T(4,128)S(1)} dynamic-update-slice(f32[16,4,384]{2,1,0:T(4,128)S(1)} %broadcast_in_dim.2, f32[16,4,256]{2,1,0:T(4,128)S(1)} %copy.32, s32[]{:T(128)} %constant.20.clone.1, s32[]{:T(128)} %constant.20.clone.1, s32[]{:T(128)S(6)} %select_n.11) | dynamic-update-slice | bytes 131076 | tf_op jit(solution)/shard_map/dynamic_update_slice | solution.py:154
  155.9 1.4 collective-permute-start.2
  157.2 5.1 %collective-permute-done.2 = bf16[16,4,128]{2,1,0:T(4,128)(2,1)S(1)} collective-permute-done((bf16[16,4,128]{2,1,0:T(4,128)(2,1)S(1)}, bf16[16,4,128]{2,1,0:T(4,128)(2,1)S(1)}, u32[]{:S(2)}, u32[]{:S(2)}) %collective-permute-start.2) | collective-permute-done | bytes 16416 | tf_op jit(solution)/shard_map/ppermute | solution.py:14
  163.2 5.7 %collective-permute-done.3 = bf16[16,4,128]{2,1,0:T(4,128)(2,1)S(1)} collective-permute-done((bf16[16,4,128]{2,1,0:T(4,128)(2,1)S(1)}, bf16[16,4,128]{2,1,0:T(4,128)(2,1)S(1)}, u32[]{:S(2)}, u32[]{:S(2)}) %collective-permute-start.3) | collective-permute-done | bytes 16416 | tf_op jit(solution)/shard_map/ppermute | solution.py:14
  168.9 0.6 fusion.48
  169.5 1.3 collective-permute-start.4
  170.8 1.3 collective-permute-start.5
  172.1 1.8 collective-permute-done.5
  174.0 1.3 collective-permute-start.6
  175.3 1.3 collective-permute-start.7
  176.6 0.3 collective-permute-done.6
  177.0 4.1 %collective-permute-done.7 = bf16[16,6,1]{2,1,0:T(8,128)(2,1)S(1)} collective-permute-done((bf16[16,6,1]{2,1,0:T(8,128)(2,1)S(1)}, bf16[16,6,1]{2,1,0:T(8,128)(2,1)S(1)}, u32[]{:S(2)}, u32[]{:S(2)}) %collective-permute-start.7) | collective-permute-done | bytes 224 | tf_op jit(solution)/shard_map/ppermute | solution.py:35
  181.1 0.1 constant_dynamic-update-slice_fusion.6
  181.2 0.1 constant_dynamic-update-slice_fusion.5
  181.4 0.1 constant_dynamic-update-slice_fusion.3
  181.5 0.1 constant_dynamic-update-slice_fusion.2
  181.7 0.1 constant_dynamic-update-slice_fusion
  181.8 1.3 multiply_convert_fusion.6
  (45 shorter events, 0.7 us)
Async XLA Ops:
  7.2 10.3 %copy-start = (bf16[304,3840]{1,0:T(8,128)(2,1)S(1)}, bf16[304,3840]{1,0:T(8,128)(2,1)}, u32[]{:S(2)}) copy-start(bf16[304,3840]{1,0:T(8,128)(2,1)} %param.16) | copy-start | bytes 7004164
  7.2 91.4 %all-reduce.2.cloned.1.call-start = ((), (), s32[]{:S(2)}) async-start(), calls=%async_computation.1 | async-start | bytes 2211840 | tf_op jit(solution)/shard_map/psum | solution.py:129
  8.2 9.9 %collective-permute-start = (bf16[16,8,128]{2,1,0:T(8,128)(2,1)S(1)}, bf16[16,8,128]{2,1,0:T(8,128)(2,1)S(1)}, u32[]{:S(2)}, u32[]{:S(2)}) collective-permute-start(bf16[16,8,128]{2,1,0:T(8,128)(2,1)S(1)} %convert_element_type.102), channel_id=1, source_target_pairs={{0,14},{2,0},{4,2},{6,4},{8,6},{10,8},{12,10},{14,12},{1,15},{3,1}... | collective-permute-start | bytes 98312 | tf_op jit(solution)/shard_map/ppermute | solution.py:14
  17.4 6.1 %copy-start.2 = (bf16[64,2432]{1,0:T(8,128)(2,1)S(1)}, bf16[64,2432]{1,0:T(8,128)(2,1)}, u32[]{:S(2)}) copy-start(bf16[64,2432]{1,0:T(8,128)(2,1)} %param.15) | copy-start | bytes 933892
  18.1 4.6 %collective-permute-start.1 = (bf16[16,8,128]{2,1,0:T(8,128)(2,1)S(1)}, bf16[16,8,128]{2,1,0:T(8,128)(2,1)S(1)}, u32[]{:S(2)}, u32[]{:S(2)}) collective-permute-start(bf16[16,8,128]{2,1,0:T(8,128)(2,1)S(1)} %collective-permute-done), channel_id=1, source_target_pairs={{0,14},{2,0},{4,2},{6,4},{8,6},{10,8},{12,10},{14,12},{1,15},{3,1}... | collective-permute-start | bytes 98312 | tf_op jit(solution)/shard_map/ppermute | solution.py:14
  24.5 2.2 %copy-start.1 = (f32[512,2432]{1,0:T(8,128)}, f32[512,2432]{1,0:T(8,128)S(1)}, u32[]{:S(2)}) copy-start(f32[512,2432]{1,0:T(8,128)S(1)} %get-tuple-element.20) | copy-start | bytes 14942212
  117.6 22.7 %slice-start = ((s8[4980736]{0:T(1024)(128)(4,1)}), s8[786432]{0:T(1024)(128)(4,1)S(1)}, s32[]{:S(2)}) async-start(s8[4980736]{0:T(1024)(128)(4,1)} %bitcast.129), calls=%async_computation.2 | async-start | bytes 1572864
  130.4 9.9 %slice-start.1 = ((s8[4980736]{0:T(1024)(128)(4,1)}), s8[4194304]{0:T(1024)(128)(4,1)S(1)}, s32[]{:S(2)}) async-start(s8[4980736]{0:T(1024)(128)(4,1)} %bitcast.129), calls=%async_computation.3 | async-start | bytes 8388608
  146.6 1.0 copy-start.3
  147.3 15.8 %copy-start.6 = (s32[128]{0:T(128)S(1)}, s32[128]{0:T(128)}, u32[]{:S(2)}) copy-start(s32[128]{0:T(128)} %param.12) | copy-start | bytes 1540
  147.3 21.6 %copy-start.4 = (f32[16,8,128]{2,1,0:T(8,128)S(1)}, f32[16,8,128]{2,1,0:T(8,128)}, u32[]{:S(2)}) copy-start(f32[16,8,128]{2,1,0:T(8,128)} %param.10) | copy-start | bytes 196612
  147.3 34.5 %copy-start.5 = (bf16[144,512]{1,0:T(8,128)(2,1)S(1)}, bf16[144,512]{1,0:T(8,128)(2,1)}, u32[]{:S(2)}) copy-start(bf16[144,512]{1,0:T(8,128)(2,1)} %param.19) | copy-start | bytes 442372
  155.9 6.5 %collective-permute-start.2 = (bf16[16,4,128]{2,1,0:T(4,128)(2,1)S(1)}, bf16[16,4,128]{2,1,0:T(4,128)(2,1)S(1)}, u32[]{:S(2)}, u32[]{:S(2)}) collective-permute-start(bf16[16,4,128]{2,1,0:T(4,128)(2,1)S(1)} %slice.194), channel_id=1, source_target_pairs={{0,2},{2,4},{4,6},{6,8},{8,10},{10,12},{12,14},{14,0},{1,3},{3,5},... | collective-permute-start | bytes 49160 | tf_op jit(solution)/shard_map/ppermute | solution.py:14
  162.4 6.5 %collective-permute-start.3 = (bf16[16,4,128]{2,1,0:T(4,128)(2,1)S(1)}, bf16[16,4,128]{2,1,0:T(4,128)(2,1)S(1)}, u32[]{:S(2)}, u32[]{:S(2)}) collective-permute-start(bf16[16,4,128]{2,1,0:T(4,128)(2,1)S(1)} %fusion.38), channel_id=1, source_target_pairs={{0,2},{2,4},{4,6},{6,8},{8,10},{10,12},{12,14},{14,0},{1,3},{3,5},... | collective-permute-start | bytes 49160 | tf_op jit(solution)/shard_map/ppermute | solution.py:14
  169.5 2.6 %collective-permute-start.4 = (bf16[16,1,128]{2,1,0:T(2,128)(2,1)S(1)}, bf16[16,1,128]{2,1,0:T(2,128)(2,1)S(1)}, u32[]{:S(2)}, u32[]{:S(2)}) collective-permute-start(bf16[16,1,128]{2,1,0:T(2,128)(2,1)S(1)} %get-tuple-element.17), channel_id=1, source_target_pairs={{0,1},{2,3},{4,5},{6,7},{8,9},{10,11},{12,13},{14,15},{16,17},{18,... | collective-permute-start | bytes 12296 | tf_op jit(solution)/shard_map/ppermute | solution.py:32
  170.8 3.1 %collective-permute-start.5 = (bf16[16,1,128]{2,1,0:T(2,128)(2,1)S(1)}, bf16[16,1,128]{2,1,0:T(2,128)(2,1)S(1)}, u32[]{:S(2)}, u32[]{:S(2)}) collective-permute-start(bf16[16,1,128]{2,1,0:T(2,128)(2,1)S(1)} %get-tuple-element.18), channel_id=1, source_target_pairs={{1,0},{3,2},{5,4},{7,6},{9,8},{11,10},{13,12},{15,14},{17,16},{19,... | collective-permute-start | bytes 12296 | tf_op jit(solution)/shard_map/ppermute | solution.py:35
  174.0 2.9 %collective-permute-start.6 = (bf16[16,6,1]{2,1,0:T(8,128)(2,1)S(1)}, bf16[16,6,1]{2,1,0:T(8,128)(2,1)S(1)}, u32[]{:S(2)}, u32[]{:S(2)}) collective-permute-start(bf16[16,6,1]{2,1,0:T(8,128)(2,1)S(1)} %get-tuple-element.15), channel_id=1, source_target_pairs={{0,2},{2,4},{4,6},{6,8},{8,10},{10,12},{12,14},{1,3},{3,5},{5,7},{... | collective-permute-start | bytes 584 | tf_op jit(solution)/shard_map/ppermute | solution.py:32
  175.3 5.8 %collective-permute-start.7 = (bf16[16,6,1]{2,1,0:T(8,128)(2,1)S(1)}, bf16[16,6,1]{2,1,0:T(8,128)(2,1)S(1)}, u32[]{:S(2)}, u32[]{:S(2)}) collective-permute-start(bf16[16,6,1]{2,1,0:T(8,128)(2,1)S(1)} %get-tuple-element.14), channel_id=1, source_target_pairs={{2,0},{4,2},{6,4},{8,6},{10,8},{12,10},{14,12},{3,1},{5,3},{7,5},{... | collective-permute-start | bytes 584 | tf_op jit(solution)/shard_map/ppermute | solution.py:35
Sparse Core Ops, SparseCore 0:
  22.2 76.3 all-reduce.1
where the time goes:
time: 191 us; the launch traced here: 190 us
  waiting for transfers between devices  88.3 us (46%)
  matrix products  37.3 us (20%)
  local copies, waits for them, and re-layouts  16.5 us (9%)
  between operations  15.8 us (8%)
  starting transfers between devices  15.4 us (8%)
  other arithmetic  12.9 us (7%)
  blocking collectives  3.79 us (2%)
    psum x1, waiting for transfers between devices, shards(): folded = lax.psum(fold(modulation, w_patch, w_qkv, place), 'width')  71.3 us
    sub x1, matrix products, attend(): weights = jax.nn.softmax(scores, axis=-1).astype(jnp.bfloat16)  12.8 us
    ppermute x4, waiting for transfers between devices, from_behind(): return lax.ppermute(x, axis, [(i, (i + by) % peers) for i in range(peers)])  10.8 us
    ppermute x4, starting transfers between devices, from_behind(): return lax.ppermute(x, axis, [(i, (i + by) % peers) for i in range(peers)])  10.2 us
    dot_general x1, matrix products, attend(): jnp.einsum('bhqk,bkhe->bqhe', weights, value_rows, preferred_element_type...  9.86 us
    add x1, local copies, waits for them, and re-layouts, shards(): projected = projected * rstd + folded[patch_rows:patch_rows + 1]  9.07 us
    dot_general x1, matrix products, shards(): mixed_out = jnp.dot(attended, w_out, preferred_element_type=jnp.float32)  6.33 us
    ppermute x2, waiting for transfers between devices, extended(): lax.ppermute(lax.slice_in_dim(block, 0, width, axis=dim), axis, backward)  5.84 us
  transfers between devices with their start and end apart: 9, of which 6 were waited for; matrix products, arithmetic and copies ran while one was open for 4% of the time, Pallas kernels for 0%

commit v1 on v0

--- a/solution.py
+++ b/solution.py
@@ -126,7 +126,7 @@
     centered = hidden - jnp.mean(hidden, axis=-1, keepdims=True)
     rstd = lax.rsqrt(jnp.mean(centered * centered, axis=-1, keepdims=True) + epsilon)
     heads = w_qkv.shape[1] // (3 * HEAD)
-    folded = lax.psum(fold(modulation, w_patch, w_qkv, place), "width")
+    folded = jnp.sum(lax.all_gather(fold(modulation, w_patch, w_qkv, place), "width"), axis=0)
     patch_rows = w_patch.shape[0]
     high, low = halves(folded[:patch_rows])
     projected = jnp.dot(

time: 191 us -> 239 us (1.25)
  waiting for transfers between devices: 88.3 us -> 134 us
    all_gather x0 -> x1, waiting for transfers between devices: none -> 113 us  [shards(): lax.all_gather(fold(modulation, w_patch, w_qkv, place), 'width')]
    psum x1 -> x0, waiting for transfers between devices: 71.3 us -> none  [shards(): folded = lax.psum(fold(modulation, w_patch, w_qkv, place), 'width')]
    reduce_sum x0 -> x1, other arithmetic: none -> 4.07 us  [shards(): jnp.sum(lax.all_gather(fold(modulation, w_patch, w_qkv, place), 'width'),...]
    ppermute x4, waiting for transfers between devices: 10.8 us -> 14.7 us  [from_behind(): return lax.ppermute(x, axis, [(i, (i + by) % peers) for i in range(peers)])]
  transfers between devices with their start and end apart: 9 -> 9, of which waited for: 6 -> 8; matrix products, arithmetic and copies ran while one was open for 4% -> 1% of each run, Pallas kernels for 0% -> 0%
where the time goes in v1:
time: 239 us
  waiting for transfers between devices  134 us (56%)
  matrix products  37.2 us (16%)
  starting transfers between devices  17 us (7%)
  between operations  15.8 us (7%)
  local copies, waits for them, and re-layouts  15.7 us (7%)
  other arithmetic  14.9 us (6%)
  blocking collectives  3.79 us (2%)
    all_gather x1, waiting for transfers between devices, shards(): lax.all_gather(fold(modulation, w_patch, w_qkv, place), 'width')  113 us
    ppermute x4, waiting for transfers between devices, from_behind(): return lax.ppermute(x, axis, [(i, (i + by) % peers) for i in range(peers)])  14.7 us
    sub x1, matrix products, attend(): weights = jax.nn.softmax(scores, axis=-1).astype(jnp.bfloat16)  12.7 us
    ppermute x4, starting transfers between devices, from_behind(): return lax.ppermute(x, axis, [(i, (i + by) % peers) for i in range(peers)])  11.8 us
    dot_general x1, matrix products, attend(): jnp.einsum('bhqk,bkhe->bqhe', weights, value_rows, preferred_element_type...  9.84 us
    add x1, local copies, waits for them, and re-layouts, shards(): projected = projected * rstd + folded[patch_rows:patch_rows + 1]  9.07 us
    dot_general x1, matrix products, shards(): mixed_out = jnp.dot(attended, w_out, preferred_element_type=jnp.float32)  6.33 us
    ppermute x2, waiting for transfers between devices, extended(): lax.ppermute(lax.slice_in_dim(block, 0, width, axis=dim), axis, backward)  5.67 us
  transfers between devices with their start and end apart: 9, of which 8 were waited for; matrix products, arithmetic and copies ran while one was open for 1% of the time, Pallas kernels for 0%

profile of v1, /device:TPU:0, one launch (start us, length us, event | category | flops | bytes accessed | tf_op | source)
XLA Modules:
  0.0 238.7 jit_solution(14106973194773137940)
XLA Ops:
  7.2 0.9 slice_reduce_fusion.1
  8.2 1.1 convert_reduce_fusion
  9.3 1.1 fusion.21
  10.4 0.1 reduce-precision_convert_fusion.1
  10.6 0.7 fusion.30
  11.3 1.2 fusion.16
  12.5 6.1 %collective-permute-start = (bf16[16,8,128]{2,1,0:T(8,128)(2,1)S(1)}, bf16[16,8,128]{2,1,0:T(8,128)(2,1)S(1)}, u32[]{:S(2)}, u32[]{:S(2)}) collective-permute-start(bf16[16,8,128]{2,1,0:T(8,128)(2,1)S(1)} %convert_element_type.102), channel_id=1, source_target_pairs={{0,14},{2,0},{4,2},{6,4},{8,6},{10,8},{12,10},{14,12},{1,15},{3,1}... | collective-permute-start | bytes 98312 | tf_op jit(solution)/shard_map/ppermute | solution.py:14
  18.6 1.6 collective-permute-done
  20.2 5.0 %collective-permute-start.1 = (bf16[16,8,128]{2,1,0:T(8,128)(2,1)S(1)}, bf16[16,8,128]{2,1,0:T(8,128)(2,1)S(1)}, u32[]{:S(2)}, u32[]{:S(2)}) collective-permute-start(bf16[16,8,128]{2,1,0:T(8,128)(2,1)S(1)} %collective-permute-done), channel_id=1, source_target_pairs={{0,14},{2,0},{4,2},{6,4},{8,6},{10,8},{12,10},{14,12},{1,15},{3,1}... | collective-permute-start | bytes 98312 | tf_op jit(solution)/shard_map/ppermute | solution.py:14
  25.9 1.5 collective-permute-done.1
  27.4 0.1 fusion.35
  27.5 0.3 copy.24
  27.8 0.4 copy.25
  28.2 0.9 fusion.52
  29.2 2.2 copy-done.2
  31.3 0.6 multiply_reduce_fusion.2
  32.0 113.4 %all-gather.4.cloned.1.call-done = f32[8,65,3840]{2,1,0:T(8,128)} async-done(((f32[1,65,3840]{2,1,0:T(8,128)}), f32[8,65,3840]{2,1,0:T(8,128)}) %all-gather.4.cloned.1.call-update) | async-done | bytes 7987216 | tf_op jit(solution)/shard_map/all_gather | solution.py:129
  145.4 4.1 %reduce_sum.82 = f32[65,3840]{1,0:T(8,128)S(1)} reduce(f32[8,65,3840]{2,1,0:T(8,128)} %all-gather.4.cloned.1.call-done, f32[]{:T(128)} %constant.19.clone.1), dimensions={0}, to_apply=%region_1.0 | reduce | flops 1747200 | bytes 8985604 | tf_op jit(solution)/shard_map/reduce_sum | solution.py:129
  149.6 4.3 %multiply_add_fusion = f32[512,3840]{1,0:T(8,128)} fusion(f32[3840]{0:T(1024)S(1)} %slice_reduce_fusion, f32[512]{0:T(512)S(1)} %add_rsqrt_fusion.3, bf16[64,3840]{1,0:T(8,128)(2,1)S(1)} %get-tuple-element.9, bf16[64,3840]{1,0:T(8,128)(2,1)S(1)} %get-tuple-element.8, bf16[512,64]{0,1:T(8,128)(2,1)S(1)} %bitcast.141), kind=kOutput, calls=%fused_computation.7 | convolution fusion | flops 509476864 | bytes 8930304 | tf_op jit(solution)/shard_map/dot_general | solution.py:132
  153.9 9.1 %copy.26 = f32[512,3840]{0,1:T(8,128)} copy(f32[512,3840]{1,0:T(8,128)} %multiply_add_fusion) | data formatting | bytes 15728640 | tf_op jit(solution)/shard_map/add | solution.py:137
  163.0 3.3 %multiply_reduce_fusion.3 = (f32[512,20]{0,1:T(8,128)S(1)}, f32[512,20]{0,1:T(8,128)S(1)}) fusion(f32[512,3,20,64]{0,3,2,1:T(8,128)} %bitcast.133), kind=kLoop, calls=%fused_computation.18 | loop fusion | flops 2600960 | bytes 5324800 | tf_op jit(solution)/shard_map/reduce_sum | solution.py:47
  166.4 12.7 %fusion.53 = (f32[20,512]{1,0:T(8,128)S(1)}, f32[20,512,512]{1,2,0:T(8,128)}) fusion(f32[512,3,20,64]{0,3,2,1:T(8,128)} %bitcast.134, f32[512,20]{0,1:T(8,128)S(1)} %get-tuple-element.26, f32[512,20]{0,1:T(8,128)S(1)} %get-tuple-element.25), kind=kOutput, calls=%fused_computation.119 | convolution fusion | flops 689439232 | bytes 26337280 | tf_op jit(solution)/shard_map/sub | solution.py:64
  179.1 9.8 %fusion.12 = bf16[20,64,512]{2,1,0:T(8,128)(2,1)S(1)} fusion(f32[20,512,512]{1,2,0:T(8,128)} %get-tuple-element.22, f32[20,512]{1,0:T(8,128)S(1)} %get-tuple-element.21, f32[512,3,20,64]{0,3,2,1:T(8,128)} %bitcast.135), kind=kOutput, calls=%fused_computation.24 | convolution fusion | flops 682229760 | bytes 23633920 | tf_op jit(solution)/shard_map/bhqk,bkhe->bqhe/dot_general | solution.py:65
  189.0 6.3 %fusion.54 = (f32[512]{0:T(512)S(1)}, f32[512,2432]{1,0:T(8,128)S(1)}) fusion(f32[512,2432]{1,0:T(8,128)S(1)} %bitcast.132, bf16[512,1280]{0,1:T(8,128)(2,1)S(1)} %bitcast.138, bf16[1280,2432]{1,0:T(8,128)(2,1)} %param.17, f32[2432]{0:T(1024)S(1)} %get-tuple-element.4), kind=kOutput, calls=%fused_computation.120 | convolution fusion | flops 3191406080 | bytes 17509888 | tf_op jit(solution)/shard_map/dot_general | solution.py:144
  195.3 0.6 multiply_reduce_fusion.1
  196.0 0.3 copy-done.4
  196.3 1.1 fusion.15
  197.4 0.4 copy.28
  197.9 0.2 copy.29
  198.1 3.8 %all_to_all.4 = bf16[1,16,8,256]{3,1,0,2:T(8,128)(2,1)S(1)} all-to-all(bf16[1,16,8,256]{3,1,0,2:T(8,128)(2,1)S(1)} %copy.29), channel_id=1, replica_groups=mesh['groups'=2,'width'=8,'guide'=2] {'guide'}, dimensions={2} | all-to-all | bytes 131072 | tf_op jit(solution)/shard_map/all_to_all | solution.py:149
  202.0 2.6 %dynamic_update_slice.3 = f32[16,4,384]{2,1,0:T(4,128)S(1)} dynamic-update-slice(f32[16,4,384]{2,1,0:T(4,128)S(1)} %broadcast_in_dim.2, f32[16,4,256]{2,1,0:T(4,128)S(1)} %copy.32, s32[]{:T(128)} %constant.20.clone.1, s32[]{:T(128)} %constant.20.clone.1, s32[]{:T(128)S(6)} %select_n.11) | dynamic-update-slice | bytes 131076 | tf_op jit(solution)/shard_map/dynamic_update_slice | solution.py:154
  204.6 0.6 collective-permute-start.2
  205.2 5.9 %collective-permute-done.2 = bf16[16,4,128]{2,1,0:T(4,128)(2,1)S(1)} collective-permute-done((bf16[16,4,128]{2,1,0:T(4,128)(2,1)S(1)}, bf16[16,4,128]{2,1,0:T(4,128)(2,1)S(1)}, u32[]{:S(2)}, u32[]{:S(2)}) %collective-permute-start.2) | collective-permute-done | bytes 16416 | tf_op jit(solution)/shard_map/ppermute | solution.py:14
  211.9 5.7 %collective-permute-done.3 = bf16[16,4,128]{2,1,0:T(4,128)(2,1)S(1)} collective-permute-done((bf16[16,4,128]{2,1,0:T(4,128)(2,1)S(1)}, bf16[16,4,128]{2,1,0:T(4,128)(2,1)S(1)}, u32[]{:S(2)}, u32[]{:S(2)}) %collective-permute-start.3) | collective-permute-done | bytes 16416 | tf_op jit(solution)/shard_map/ppermute | solution.py:14
  217.6 0.6 fusion.49
  218.2 1.3 collective-permute-start.4
  219.5 1.3 collective-permute-start.5
  220.8 1.8 collective-permute-done.5
  222.7 1.3 collective-permute-start.6
  224.0 1.3 collective-permute-start.7
  225.3 0.4 collective-permute-done.6
  225.9 3.9 %collective-permute-done.7 = bf16[16,6,1]{2,1,0:T(8,128)(2,1)S(1)} collective-permute-done((bf16[16,6,1]{2,1,0:T(8,128)(2,1)S(1)}, bf16[16,6,1]{2,1,0:T(8,128)(2,1)S(1)}, u32[]{:S(2)}, u32[]{:S(2)}) %collective-permute-start.7) | collective-permute-done | bytes 224 | tf_op jit(solution)/shard_map/ppermute | solution.py:35
  229.8 0.1 constant_dynamic-update-slice_fusion.6
  229.9 0.1 constant_dynamic-update-slice_fusion.5
  230.1 0.1 constant_dynamic-update-slice_fusion.3
  230.2 0.1 constant_dynamic-update-slice_fusion.2
  230.4 0.1 constant_dynamic-update-slice_fusion
  230.5 1.3 multiply_convert_fusion.6
  (48 shorter events, 0.8 us)
Async XLA Ops:
  7.2 3.4 %copy-start = (bf16[304,3840]{1,0:T(8,128)(2,1)S(1)}, bf16[304,3840]{1,0:T(8,128)(2,1)}, u32[]{:S(2)}) copy-start(bf16[304,3840]{1,0:T(8,128)(2,1)} %param.16) | copy-start | bytes 7004164
  7.2 138.2 %all-gather.4.cloned.1.call-start = ((), (), s32[]{:S(2)}) async-start(), calls=%async_computation.1 | async-start | bytes 9953280 | tf_op jit(solution)/shard_map/all_gather | solution.py:129
  10.4 2.1 copy-start.5
  10.6 17.6 %copy-start.3 = (bf16[64,2432]{1,0:T(8,128)(2,1)S(1)}, bf16[64,2432]{1,0:T(8,128)(2,1)}, u32[]{:S(2)}) copy-start(bf16[64,2432]{1,0:T(8,128)(2,1)} %param.15) | copy-start | bytes 933892
  12.5 7.7 %collective-permute-start = (bf16[16,8,128]{2,1,0:T(8,128)(2,1)S(1)}, bf16[16,8,128]{2,1,0:T(8,128)(2,1)S(1)}, u32[]{:S(2)}, u32[]{:S(2)}) collective-permute-start(bf16[16,8,128]{2,1,0:T(8,128)(2,1)S(1)} %convert_element_type.102), channel_id=1, source_target_pairs={{0,14},{2,0},{4,2},{6,4},{8,6},{10,8},{12,10},{14,12},{1,15},{3,1}... | collective-permute-start | bytes 98312 | tf_op jit(solution)/shard_map/ppermute | solution.py:14
  20.2 7.2 %collective-permute-start.1 = (bf16[16,8,128]{2,1,0:T(8,128)(2,1)S(1)}, bf16[16,8,128]{2,1,0:T(8,128)(2,1)S(1)}, u32[]{:S(2)}, u32[]{:S(2)}) collective-permute-start(bf16[16,8,128]{2,1,0:T(8,128)(2,1)S(1)} %collective-permute-done), channel_id=1, source_target_pairs={{0,14},{2,0},{4,2},{6,4},{8,6},{10,8},{12,10},{14,12},{1,15},{3,1}... | collective-permute-start | bytes 98312 | tf_op jit(solution)/shard_map/ppermute | solution.py:14
  29.1 2.2 copy-start.2
  166.4 22.6 %slice-start = ((s8[4980736]{0:T(1024)(128)(4,1)}), s8[786432]{0:T(1024)(128)(4,1)S(1)}, s32[]{:S(2)}) async-start(s8[4980736]{0:T(1024)(128)(4,1)} %bitcast.131), calls=%async_computation.2 | async-start | bytes 1572864
  179.1 9.9 %slice-start.1 = ((s8[4980736]{0:T(1024)(128)(4,1)}), s8[4194304]{0:T(1024)(128)(4,1)S(1)}, s32[]{:S(2)}) async-start(s8[4980736]{0:T(1024)(128)(4,1)} %bitcast.131), calls=%async_computation.3 | async-start | bytes 8388608
  195.3 1.0 copy-start.4
  196.0 15.8 %copy-start.7 = (s32[128]{0:T(128)S(1)}, s32[128]{0:T(128)}, u32[]{:S(2)}) copy-start(s32[128]{0:T(128)} %param.12) | copy-start | bytes 1540
  196.0 34.5 %copy-start.6 = (bf16[144,512]{1,0:T(8,128)(2,1)S(1)}, bf16[144,512]{1,0:T(8,128)(2,1)}, u32[]{:S(2)}) copy-start(bf16[144,512]{1,0:T(8,128)(2,1)} %param.19) | copy-start | bytes 442372
  196.3 35.5 %copy-start.1 = (bf16[304,3840]{1,0:T(8,128)(2,1)S(1)}, bf16[304,3840]{1,0:T(8,128)(2,1)}, u32[]{:S(2)}) copy-start(bf16[304,3840]{1,0:T(8,128)(2,1)} %param.16) | copy-start | bytes 7004164
  204.6 6.5 %collective-permute-start.2 = (bf16[16,4,128]{2,1,0:T(4,128)(2,1)S(1)}, bf16[16,4,128]{2,1,0:T(4,128)(2,1)S(1)}, u32[]{:S(2)}, u32[]{:S(2)}) collective-permute-start(bf16[16,4,128]{2,1,0:T(4,128)(2,1)S(1)} %slice.196), channel_id=1, source_target_pairs={{0,2},{2,4},{4,6},{6,8},{8,10},{10,12},{12,14},{14,0},{1,3},{3,5},... | collective-permute-start | bytes 49160 | tf_op jit(solution)/shard_map/ppermute | solution.py:14
  211.1 6.5 %collective-permute-start.3 = (bf16[16,4,128]{2,1,0:T(4,128)(2,1)S(1)}, bf16[16,4,128]{2,1,0:T(4,128)(2,1)S(1)}, u32[]{:S(2)}, u32[]{:S(2)}) collective-permute-start(bf16[16,4,128]{2,1,0:T(4,128)(2,1)S(1)} %fusion.39), channel_id=1, source_target_pairs={{0,2},{2,4},{4,6},{6,8},{8,10},{10,12},{12,14},{14,0},{1,3},{3,5},... | collective-permute-start | bytes 49160 | tf_op jit(solution)/shard_map/ppermute | solution.py:14
  218.2 2.6 %collective-permute-start.4 = (bf16[16,1,128]{2,1,0:T(2,128)(2,1)S(1)}, bf16[16,1,128]{2,1,0:T(2,128)(2,1)S(1)}, u32[]{:S(2)}, u32[]{:S(2)}) collective-permute-start(bf16[16,1,128]{2,1,0:T(2,128)(2,1)S(1)} %get-tuple-element.17), channel_id=1, source_target_pairs={{0,1},{2,3},{4,5},{6,7},{8,9},{10,11},{12,13},{14,15},{16,17},{18,... | collective-permute-start | bytes 12296 | tf_op jit(solution)/shard_map/ppermute | solution.py:32
  219.5 3.1 %collective-permute-start.5 = (bf16[16,1,128]{2,1,0:T(2,128)(2,1)S(1)}, bf16[16,1,128]{2,1,0:T(2,128)(2,1)S(1)}, u32[]{:S(2)}, u32[]{:S(2)}) collective-permute-start(bf16[16,1,128]{2,1,0:T(2,128)(2,1)S(1)} %get-tuple-element.18), channel_id=1, source_target_pairs={{1,0},{3,2},{5,4},{7,6},{9,8},{11,10},{13,12},{15,14},{17,16},{19,... | collective-permute-start | bytes 12296 | tf_op jit(solution)/shard_map/ppermute | solution.py:35
  222.7 3.0 %collective-permute-start.6 = (bf16[16,6,1]{2,1,0:T(8,128)(2,1)S(1)}, bf16[16,6,1]{2,1,0:T(8,128)(2,1)S(1)}, u32[]{:S(2)}, u32[]{:S(2)}) collective-permute-start(bf16[16,6,1]{2,1,0:T(8,128)(2,1)S(1)} %get-tuple-element.15), channel_id=1, source_target_pairs={{0,2},{2,4},{4,6},{6,8},{8,10},{10,12},{12,14},{1,3},{3,5},{5,7},{... | collective-permute-start | bytes 584 | tf_op jit(solution)/shard_map/ppermute | solution.py:32
  224.0 5.8 %collective-permute-start.7 = (bf16[16,6,1]{2,1,0:T(8,128)(2,1)S(1)}, bf16[16,6,1]{2,1,0:T(8,128)(2,1)S(1)}, u32[]{:S(2)}, u32[]{:S(2)}) collective-permute-start(bf16[16,6,1]{2,1,0:T(8,128)(2,1)S(1)} %get-tuple-element.14), channel_id=1, source_target_pairs={{2,0},{4,2},{6,4},{8,6},{10,8},{12,10},{14,12},{3,1},{5,3},{7,5},{... | collective-permute-start | bytes 584 | tf_op jit(solution)/shard_map/ppermute | solution.py:35
Sparse Core Ops, SparseCore 0:
  12.6 132.7 all-gather.3
